TPU v7x, 128 devices: a whole 4x4x4 slice. The times are simulated.
128 devices in a mesh: rep: 2 (over x_hi), fsdp: 16 (over y, x_lo, core), tp: 4 (over z).
Axes of the slice: x: 4 (x_hi: 2, x_lo: 2; x = x_hi * 2 + x_lo), y: 4, z: 4, core: 2. Of those that a mesh axis runs over, the one named last changes fastest.
Arguments:
- gate_up_master: float32 [2, 4096, 14336], P(None, 'fsdp', ('rep', 'tp')), may hold values from -0.09375 to 0.09375
- gate_up_moment: float32 [2, 4096, 14336], P(None, 'fsdp', ('rep', 'tp')), may hold values from -0.00018310547 to 0.00018310547
- gate_up_second: float32 [2, 4096, 14336], P(None, 'fsdp', ('rep', 'tp')), may hold values from 8.5149493e-10 to 8.51495e-09
- gate_up_grad: bfloat16 [2, 4096, 14336], P(None, 'fsdp', ('rep', 'tp')), may hold values from -8 to 8
- down_master: float32 [4096, 14336], P('fsdp', ('rep', 'tp')), may hold values from -0.046875 to 0.046875
- down_moment: float32 [4096, 14336], P('fsdp', ('rep', 'tp')), may hold values from -0.00018310547 to 0.00018310547
- down_second: float32 [4096, 14336], P('fsdp', ('rep', 'tp')), may hold values from 8.5149493e-10 to 8.51495e-09
- down_grad: bfloat16 [4096, 14336], P('fsdp', ('rep', 'tp')), may hold values from -8 to 8
- norm_gain: float32 [4096], replicated, may hold values from 0.1 to 1.9
- start_rows: bfloat16 [1024, 4096], P(('rep', 'fsdp', 'tp')), may hold values from -6 to 6
- queries: bfloat16 [2, 1024, 4096], P(None, ('rep', 'fsdp', 'tp')), may hold values from -6 to 6
- new_kv: bfloat16 [2, 1024, 2, 1024], P(None, ('rep', 'fsdp', 'tp')), may hold values from -6 to 6
- kv_pool: bfloat16 [8192, 16, 2, 1024], P(('rep', 'fsdp', 'tp')), may hold values from -6 to 6
- page_table: int32 [1024, 8], P(('rep', 'fsdp', 'tp')), may hold values from 0 to 63, as said below
- cache_len: int32 [1024], P(('rep', 'fsdp', 'tp')), may hold values from 1 to 128, as said below
Outputs:
- final_rows: bfloat16 [1024, 4096], P(('rep', 'fsdp', 'tp'))
Inputs may be any that keep to these rules, and one draw needn't show every extreme that they name: `page_table`: within each aligned block of 8 rows, the entries name each of the 64 pages of that block exactly once. `cache_len`: some row has exactly 128 cached positions.
All inputs are finite; a program needn't handle non-finite values.
Results may differ from a plain program's by a relative error of at most 0.019.
Values may be sent and summed in bfloat16 or wider, within the bound.
No kernel may reach another device: no remote copies, remote signals or barrier semaphores. Data moves between devices by JAX's collectives and lax.ppermute only.
A program may use at most 128 MiB of HBM per device.

v0:
```python
import jax
import jax.numpy as jnp
from jax import lax
from jax.sharding import PartitionSpec as P

D = 4096
HD = 128
beta_one = 0.9
beta_two = 0.95
adam_eps = 1e-08
adam_time = 100.0
norm_eps = 1e-05


def adam_new(master, moment, second, grad, clip):
    learn_rate = 2.0 / D**0.5
    g = grad.astype(jnp.float32) * clip
    m = beta_one * moment + (1.0 - beta_one) * g
    v = beta_two * second + (1.0 - beta_two) * g * g
    first_fix = 1.0 - beta_one**adam_time
    second_fix = 1.0 - beta_two**adam_time
    return (master - learn_rate * (m / first_fix) / (jnp.sqrt(v / second_fix) + adam_eps)).astype(
        jnp.bfloat16
    )


def attend(query, keys, values, valid, fresh_k, fresh_v, step):
    scale = query.shape[-1] ** (-0.5)
    old = jnp.einsum("rjgh,rcjh->rjgc", query, keys, preferred_element_type=jnp.float32) * scale
    old = jnp.where(valid[:, None, None, :], old, -1e30)
    new = jnp.einsum("rjgh,srjh->rjgs", query, fresh_k, preferred_element_type=jnp.float32) * scale
    allowed = jnp.arange(fresh_k.shape[0]) <= step
    new = jnp.where(allowed[None, None, None, :], new, -1e30)
    top = jnp.maximum(jnp.max(old, axis=-1, keepdims=True), jnp.max(new, axis=-1, keepdims=True))
    exp_old = jnp.exp(old - top)
    exp_new = jnp.exp(new - top)
    total = jnp.sum(exp_old, axis=-1, keepdims=True) + jnp.sum(exp_new, axis=-1, keepdims=True)
    prob_old = (exp_old / total).astype(jnp.bfloat16)
    prob_new = (exp_new / total).astype(jnp.bfloat16)
    out = jnp.einsum("rjgc,rcjh->rjgh", prob_old, values, preferred_element_type=jnp.float32)
    out = out + jnp.einsum("rjgs,srjh->rjgh", prob_new, fresh_v, preferred_element_type=jnp.float32)
    return out.reshape(out.shape[0], -1)


def shards(
    gate_up_master,
    gate_up_moment,
    gate_up_second,
    gate_up_grad,
    down_master,
    down_moment,
    down_second,
    down_grad,
    norm_gain,
    start_rows,
    queries,
    new_kv,
    kv_pool,
    page_table,
    cache_len,
):
    local_squares = jnp.sum(jnp.square(gate_up_grad.astype(jnp.float32))) + jnp.sum(
        jnp.square(down_grad.astype(jnp.float32))
    )
    total = lax.psum(local_squares, ("rep", "fsdp", "tp"))
    clip = jnp.minimum(1.0, 1.0 / jnp.sqrt(total))
    gate_up = adam_new(gate_up_master, gate_up_moment, gate_up_second, gate_up_grad, clip)
    down_t = adam_new(down_master, down_moment, down_second, down_grad, clip)[None]
    n_fsdp = lax.axis_size("fsdp")
    n_rep = lax.axis_size("rep")
    cols = gate_up.shape[2]
    copied = (
        lax.all_gather(gate_up, "rep", axis=2, tiled=True),
        lax.all_gather(down_t, "rep", axis=2, tiled=True),
    )
    shaped = tuple(
        (a.reshape(a.shape[0], a.shape[1], n_rep, n_fsdp, cols // n_fsdp) for a in copied)
    )
    moved = (
        lax.all_to_all(shaped[0], "fsdp", split_axis=3, concat_axis=1, tiled=True),
        lax.all_to_all(shaped[1], "fsdp", split_axis=3, concat_axis=1, tiled=True),
    )
    weights = tuple((a.reshape(a.shape[0], a.shape[1], -1) for a in moved))
    roll_gate_up = weights[0]
    roll_down = weights[1][0]
    local_rows = start_rows.shape[0]
    kv_width = new_kv.shape[-1]
    head_dim = HD
    key_heads = kv_width // head_dim
    cache = kv_pool[page_table].reshape(local_rows, -1, 2, key_heads, head_dim)
    keys = cache[:, :, 0]
    values = cache[:, :, 1]
    valid = jnp.arange(keys.shape[1], dtype=jnp.int32)[None, :] < cache_len[:, None]
    fresh = new_kv.reshape(new_kv.shape[0], local_rows, 2, key_heads, head_dim)
    fresh_k = fresh[:, :, 0]
    fresh_v = fresh[:, :, 1]
    rows = start_rows
    for step in range(queries.shape[0]):
        query = queries[step].reshape(local_rows, key_heads, -1, head_dim)
        attended = attend(query, keys, values, valid, fresh_k, fresh_v, step)
        mixed = (rows.astype(jnp.float32) + attended).astype(jnp.bfloat16)
        mixed_f = mixed.astype(jnp.float32)
        normed = (
            mixed_f
            * lax.rsqrt(jnp.mean(mixed_f * mixed_f, axis=-1, keepdims=True) + norm_eps)
            * norm_gain
        ).astype(jnp.bfloat16)
        whole = lax.all_gather(normed, ("fsdp", "tp"), axis=0, tiled=True)
        gate = jnp.dot(whole, roll_gate_up[0], preferred_element_type=jnp.float32)
        upper = jnp.dot(whole, roll_gate_up[1], preferred_element_type=jnp.float32)
        hidden = (jax.nn.silu(gate) * upper).astype(jnp.bfloat16)
        summed = lax.psum_scatter(
            lax.dot_general(
                hidden, roll_down, (((1,), (1,)), ((), ())), preferred_element_type=jnp.float32
            ),
            ("fsdp", "tp"),
            scatter_dimension=0,
            tiled=True,
        )
        rows = (mixed_f + summed).astype(jnp.bfloat16)
    return rows


def solution(mesh):
    in_specs = (
        P(None, "fsdp", ("rep", "tp")),
        P(None, "fsdp", ("rep", "tp")),
        P(None, "fsdp", ("rep", "tp")),
        P(None, "fsdp", ("rep", "tp")),
        P("fsdp", ("rep", "tp")),
        P("fsdp", ("rep", "tp")),
        P("fsdp", ("rep", "tp")),
        P("fsdp", ("rep", "tp")),
        P(),
        P(("rep", "fsdp", "tp"), None),
        P(None, ("rep", "fsdp", "tp"), None),
        P(None, ("rep", "fsdp", "tp"), None, None),
        P(("rep", "fsdp", "tp"), None, None, None),
        P(("rep", "fsdp", "tp"), None),
        P(("rep", "fsdp", "tp")),
    )
    out_specs = P(("rep", "fsdp", "tp"), None)
    return jax.shard_map(shards, mesh=mesh, in_specs=in_specs, out_specs=out_specs, check_vma=False)
```

profile of v0, /device:TPU:0, one launch (start us, length us, event | category | flops | bytes accessed | tf_op | source)
XLA Modules:
  0.0 1184.5 jit_solution(11952147557319080114)
XLA Ops:
  9.1 2.8 copy.40
  14.8 68.2 %psum.7 = f32[]{:T(128)} all-reduce(f32[]{:T(128)S(6)} %add.102), channel_id=1, replica_groups=mesh['rep'=2,'fsdp'=16,'tp'=4] {'rep','fsdp','tp'}, use_global_device_ids=true, to_apply=%region_7.8 | all-reduce | flops 1 | bytes 8 | tf_op jit(solution)/shard_map/psum | solution.py:65
  83.7 2.8 copy.49
  86.5 2.8 copy.47
  89.2 2.7 copy.48
  91.9 5.0 fusion.25
  97.0 5.1 copy.43
  102.2 5.3 copy.39
  107.5 5.1 copy.42
  112.6 6.7 fusion.10
  119.8 12.9 %gather_fusion = bf16[64,16,2,1024]{3,2,1,0:T(2,128)(2,1)} fusion(bf16[64,16,2,1024]{3,2,1,0:T(2,128)(2,1)} %param.27, s32[1024]{0:T(1024)S(1)} %pad_clamp_fusion), kind=kCustom, calls=%fused_computation | custom fusion | bytes 8388864 | tf_op jit(solution)/shard_map/gather | solution.py:90
  132.7 7.8 reshape.110
  140.9 2.9 fusion.72
  147.6 2.9 copy.50
  150.6 3.7 all-to-all-start.1
  154.3 48.9 %all-gather.8.cloned.1.call-done = bf16[2,256,3584]{1,2,0:T(8,128)(2,1)} async-done(((bf16[2,256,1792]{1,2,0:T(8,128)(2,1)}), bf16[2,256,3584]{1,2,0:T(8,128)(2,1)}) %all-gather.8.cloned.1.call-update) | async-done | bytes 3670032 | tf_op jit(solution)/shard_map/all_gather | solution.py:73
  203.1 4.4 copy.44
  207.5 4.5 all-to-all-start
  214.2 45.9 %all-to-all-done = bf16[2,256,2,16,112]{1,4,2,0,3:T(8,128)(2,1)} async-done(((bf16[2,256,2,16,112]{1,4,2,0,3:T(8,128)(2,1)}), bf16[2,256,2,16,112]{1,4,2,0,3:T(8,128)(2,1)}, u32[]{:S(2)}, u32[]{:S(2)}) %all-to-all-start) | async-done | bytes 3670048 | tf_op jit(solution)/shard_map/all_to_all | solution.py:80
  260.1 2.3 fusion.73
  263.4 2.1 copy.62
  266.5 2.1 copy.63
  268.6 124.0 %all-gather.6.cloned.1.call-done = bf16[512,4096]{1,0:T(8,128)(2,1)} async-done(((bf16[8,4096]{1,0:T(8,128)(2,1)}), bf16[512,4096]{1,0:T(8,128)(2,1)}) %all-gather.6.cloned.1.call-update) | async-done | bytes 4194320 | tf_op jit(solution)/shard_map/all_gather | solution.py:108
  392.6 4.2 fusion.80
  396.9 8.7 fusion.27
  405.9 3.0 fusion.76
  410.4 294.7 %reduce-scatter.3.cloned.1.call-done = f32[8,4096]{1,0:T(8,128)} async-done(((f32[512,4096]{1,0:T(8,128)}), f32[8,4096]{1,0:T(8,128)}) %reduce-scatter.3.cloned.1.call-update) | async-done | bytes 131088 | tf_op jit(solution)/shard_map/reduce_scatter | solution.py:112
  707.3 156.1 %all-gather.10.cloned.1.call-done = bf16[512,4096]{1,0:T(8,128)(2,1)} async-done(((bf16[8,4096]{1,0:T(8,128)(2,1)}), bf16[512,4096]{1,0:T(8,128)(2,1)}) %all-gather.10.cloned.1.call-update) | async-done | bytes 4194320 | tf_op jit(solution)/shard_map/all_gather | solution.py:108
  863.4 4.2 fusion.81
  867.6 8.8 fusion.29
  876.5 299.7 %reduce-scatter.5.cloned.1.call-done = f32[8,4096]{1,0:T(8,128)} async-done(((f32[512,4096]{1,0:T(8,128)}), f32[8,4096]{1,0:T(8,128)}) %reduce-scatter.5.cloned.1.call-update) | async-done | bytes 131088 | tf_op jit(solution)/shard_map/reduce_scatter | solution.py:112
  1176.1 1.5 fusion.59
  (73 shorter events, 16.7 us)
Async XLA Ops:
  6.5 141.1 %all-gather.12.cloned.1.call-start = ((), (), s32[]{:S(2)}) async-start(), calls=%async_computation.9 | async-start | bytes 2752512 | tf_op jit(solution)/shard_map/all_gather | solution.py:74
  97.0 106.2 %all-gather.8.cloned.1.call-start = ((), (), s32[]{:S(2)}) async-start(), calls=%async_computation.5 | async-start | bytes 5505024 | tf_op jit(solution)/shard_map/all_gather | solution.py:73
  112.6 7.0 copy-start.7
  112.6 7.1 copy-start.5
  112.6 7.1 copy-start.3
  119.3 273.3 %all-gather.6.cloned.1.call-start = ((), (), s32[]{:S(2)}) async-start(), calls=%async_computation.4 | async-start | bytes 4259840 | tf_op jit(solution)/shard_map/all_gather | solution.py:108
  132.7 7.8 copy-start.8
  143.9 2.0 copy-start.2
  143.9 2.0 copy-start
  145.9 0.8 copy-start.6
  145.9 1.0 copy-start.4
  150.6 56.9 %all-to-all-start.1 = ((bf16[1,256,2,16,112]{1,4,2,0,3:T(8,128)(2,1)}), bf16[1,256,2,16,112]{1,4,2,0,3:T(8,128)(2,1)S(1)}, u32[]{:S(2)}, u32[]{:S(2)}) async-start(bf16[1,256,2,16,112]{1,4,2,0,3:T(8,128)(2,1)} %copy.50), calls=%async_computation.1 | async-start | bytes 3670016 | tf_op jit(solution)/shard_map/all_to_all | solution.py:81
  207.5 52.5 %all-to-all-start = ((bf16[2,256,2,16,112]{1,4,2,0,3:T(8,128)(2,1)}), bf16[2,256,2,16,112]{1,4,2,0,3:T(8,128)(2,1)}, u32[]{:S(2)}, u32[]{:S(2)}) async-start(bf16[2,256,2,16,112]{1,4,2,0,3:T(8,128)(2,1)} %copy.44), calls=%async_computation | async-start | bytes 7340032 | tf_op jit(solution)/shard_map/all_to_all | solution.py:80
  212.1 493.1 %reduce-scatter.3.cloned.1.call-start = ((), (), s32[]{:S(2)}) async-start(), calls=%async_computation.6 | async-start | bytes 8519680 | tf_op jit(solution)/shard_map/reduce_scatter | solution.py:112
  405.5 457.9 %all-gather.10.cloned.1.call-start = ((), (), s32[]{:S(2)}) async-start(), calls=%async_computation.7 | async-start | bytes 4259840 | tf_op jit(solution)/shard_map/all_gather | solution.py:108
  405.9 3.7 copy-start.1
  707.0 469.2 %reduce-scatter.5.cloned.1.call-start = ((), (), s32[]{:S(2)}) async-start(), calls=%async_computation.8 | async-start | bytes 8519680 | tf_op jit(solution)/shard_map/reduce_scatter | solution.py:112
Sparse Core Ops, SparseCore 0:
  97.1 30.3 all-gather.11
  129.1 73.9 all-gather.7
  204.8 187.7 all-gather.5
  405.7 299.4 reduce-scatter.2
  707.1 156.2 all-gather.9
  876.6 299.5 reduce-scatter.4
where the time goes:
time: 1190 us; the launch traced here: 1180 us
  waiting for transfers between devices  969 us (81%)
  local copies, waits for them, and re-layouts  69.8 us (6%)
  blocking collectives  68.2 us (6%)
  matrix products  32.6 us (3%)
  other arithmetic  19.5 us (2%)
  between operations  15.8 us (1%)
    reduce_scatter x2, waiting for transfers between devices, shards(): lax.psum_scatter(lax.dot_general(hidden, roll_down, (((1,), (1,)), ((), (...  594 us
    all_gather x2, waiting for transfers between devices, shards(): whole = lax.all_gather(normed, ('fsdp', 'tp'), axis=0, tiled=True)  280 us
    psum x1, blocking collectives, shards(): total = lax.psum(local_squares, ('rep', 'fsdp', 'tp'))  68.2 us
    all_gather x1, waiting for transfers between devices, shards(): lax.all_gather(gate_up, 'rep', axis=2, tiled=True)  48.9 us
    all_to_all x1, waiting for transfers between devices, shards(): lax.all_to_all(shaped[0], 'fsdp', split_axis=3, concat_axis=1, tiled=True)  45.9 us
    unnamed x29, local copies, waits for them, and re-layouts  33.1 us
  transfers between devices with their start and end apart: 8, of which 6 were waited for; matrix products, arithmetic and copies ran while one was open for 6% of the time, Pallas kernels for 0%

commit v1 on v0

--- a/solution.py
+++ b/solution.py
@@ -70,7 +70,9 @@
     n_rep = lax.axis_size("rep")
     cols = gate_up.shape[2]
     copied = (
-        lax.all_gather(gate_up, "rep", axis=2, tiled=True),
+        jnp.concatenate(
+            lax.all_to_all(jnp.stack([gate_up] * lax.axis_size("rep")), "rep", 0, 0), axis=2
+        ),
         lax.all_gather(down_t, "rep", axis=2, tiled=True),
     )
     shaped = tuple(

time: 1190 us -> 1130 us (0.950)
  waiting for transfers between devices: 969 us -> 904 us
    all_gather x2, waiting for transfers between devices: 280 us -> 193 us  [shards(): whole = lax.all_gather(normed, ('fsdp', 'tp'), axis=0, tiled=True)]
    all_gather x1 -> x0, waiting for transfers between devices: 48.9 us -> none  [shards(): lax.all_gather(gate_up, 'rep', axis=2, tiled=True)]
    all_to_all x0 -> x1, waiting for transfers between devices: none -> 46.3 us  [shards(): lax.all_to_all(jnp.stack([gate_up] * lax.axis_size('rep')), 'rep', 0, 0)]
    all_to_all x1, waiting for transfers between devices: 0.01 us -> 23.2 us  [shards(): lax.all_to_all(shaped[1], 'fsdp', split_axis=3, concat_axis=1, tiled=True)]
  transfers between devices with their start and end apart: 8 -> 8, of which waited for: 6 -> 7; matrix products, arithmetic and copies ran while one was open for 6% -> 6% of each run, Pallas kernels for 0% -> 0%
where the time goes in v1:
time: 1130 us; the launch traced here: 1120 us
  waiting for transfers between devices  904 us (80%)
  local copies, waits for them, and re-layouts  68.9 us (6%)
  blocking collectives  68.2 us (6%)
  matrix products  32.5 us (3%)
  other arithmetic  20.8 us (2%)
  between operations  15.5 us (1%)
  starting transfers between devices  14.5 us (1%)
    reduce_scatter x2, waiting for transfers between devices, shards(): lax.psum_scatter(lax.dot_general(hidden, roll_down, (((1,), (1,)), ((), (...  596 us
    all_gather x2, waiting for transfers between devices, shards(): whole = lax.all_gather(normed, ('fsdp', 'tp'), axis=0, tiled=True)  193 us
    psum x1, blocking collectives, shards(): total = lax.psum(local_squares, ('rep', 'fsdp', 'tp'))  68.2 us
    all_to_all x1, waiting for transfers between devices, shards(): lax.all_to_all(jnp.stack([gate_up] * lax.axis_size('rep')), 'rep', 0, 0)  46.3 us
    all_to_all x1, waiting for transfers between devices, shards(): lax.all_to_all(shaped[0], 'fsdp', split_axis=3, concat_axis=1, tiled=True)  45.4 us
    unnamed x29, local copies, waits for them, and re-layouts  32.9 us
    all_to_all x1, waiting for transfers between devices, shards(): lax.all_to_all(shaped[1], 'fsdp', split_axis=3, concat_axis=1, tiled=True)  23.2 us
  transfers between devices with their start and end apart: 8, of which 7 were waited for; matrix products, arithmetic and copies ran while one was open for 6% of the time, Pallas kernels for 0%

profile of v1, /device:TPU:0, one launch (start us, length us, event | category | flops | bytes accessed | tf_op | source)
XLA Modules:
  0.0 1124.4 jit_solution(13555531739420903412)
XLA Ops:
  9.1 2.8 copy.40
  14.8 68.2 %psum.7 = f32[]{:T(128)} all-reduce(f32[]{:T(128)S(6)} %add.102), channel_id=1, replica_groups=mesh['rep'=2,'fsdp'=16,'tp'=4] {'rep','fsdp','tp'}, use_global_device_ids=true, to_apply=%region_7.8 | all-reduce | flops 1 | bytes 8 | tf_op jit(solution)/shard_map/psum | solution.py:65
  83.7 2.8 copy.50
  86.5 2.7 copy.48
  89.2 2.7 copy.49
  92.0 5.1 fusion.25
  97.7 12.9 %gather_fusion = bf16[64,16,2,1024]{3,2,1,0:T(2,128)(2,1)} fusion(bf16[64,16,2,1024]{3,2,1,0:T(2,128)(2,1)} %param.27, s32[1024]{0:T(1024)S(1)} %pad_clamp_fusion), kind=kCustom, calls=%fused_computation | custom fusion | bytes 8388864 | tf_op jit(solution)/shard_map/gather | solution.py:92
  110.6 7.6 reshape.110
  118.2 2.5 fusion.73
  124.7 5.1 copy.43
  129.8 5.1 copy.39
  135.0 5.1 copy.42
  140.1 5.7 fusion.26
  145.8 2.1 pad_maximum_fusion
  148.0 5.4 all-to-all-start
  153.4 2.9 copy.51
  156.3 46.3 %all-to-all-done = bf16[2,2,256,1792]{2,3,1,0:T(8,128)(2,1)} async-done(((bf16[2,2,256,1792]{2,3,1,0:T(8,128)(2,1)}), bf16[2,2,256,1792]{2,3,1,0:T(8,128)(2,1)}, u32[]{:S(2)}, u32[]{:S(2)}) %all-to-all-start) | async-done | bytes 3670048 | tf_op jit(solution)/shard_map/all_to_all | solution.py:74
  202.7 3.7 all-to-all-start.2
  206.4 4.3 copy.45
  210.7 23.2 %all-to-all-done.2 = bf16[1,256,2,16,112]{1,4,2,0,3:T(8,128)(2,1)S(1)} async-done(((bf16[1,256,2,16,112]{1,4,2,0,3:T(8,128)(2,1)}), bf16[1,256,2,16,112]{1,4,2,0,3:T(8,128)(2,1)S(1)}, u32[]{:S(2)}, u32[]{:S(2)}) %all-to-all-start.2) | async-done | bytes 1835040 | tf_op jit(solution)/shard_map/all_to_all | solution.py:83
  233.9 4.5 all-to-all-start.1
  240.6 45.4 %all-to-all-done.1 = bf16[2,256,2,16,112]{1,4,2,0,3:T(8,128)(2,1)} async-done(((bf16[2,256,2,16,112]{1,4,2,0,3:T(8,128)(2,1)}), bf16[2,256,2,16,112]{1,4,2,0,3:T(8,128)(2,1)}, u32[]{:S(2)}, u32[]{:S(2)}) %all-to-all-start.1) | async-done | bytes 3670048 | tf_op jit(solution)/shard_map/all_to_all | solution.py:82
  285.9 2.3 fusion.74
  294.4 37.3 %all-gather.5.cloned.1.call-done = bf16[512,4096]{1,0:T(8,128)(2,1)} async-done(((bf16[8,4096]{1,0:T(8,128)(2,1)}), bf16[512,4096]{1,0:T(8,128)(2,1)}) %all-gather.5.cloned.1.call-update) | async-done | bytes 4194320 | tf_op jit(solution)/shard_map/all_gather | solution.py:110
  331.7 4.2 fusion.81
  335.9 8.7 fusion.28
  345.0 3.0 fusion.77
  349.5 296.4 %reduce-scatter.3.cloned.1.call-done = f32[8,4096]{1,0:T(8,128)} async-done(((f32[512,4096]{1,0:T(8,128)}), f32[8,4096]{1,0:T(8,128)}) %reduce-scatter.3.cloned.1.call-update) | async-done | bytes 131088 | tf_op jit(solution)/shard_map/reduce_scatter | solution.py:114
  648.0 155.7 %all-gather.7.cloned.1.call-done = bf16[512,4096]{1,0:T(8,128)(2,1)} async-done(((bf16[8,4096]{1,0:T(8,128)(2,1)}), bf16[512,4096]{1,0:T(8,128)(2,1)}) %all-gather.7.cloned.1.call-update) | async-done | bytes 4194320 | tf_op jit(solution)/shard_map/all_gather | solution.py:110
  803.7 4.2 fusion.82
  807.9 8.7 fusion.30
  816.6 299.7 %reduce-scatter.5.cloned.1.call-done = f32[8,4096]{1,0:T(8,128)} async-done(((f32[512,4096]{1,0:T(8,128)}), f32[8,4096]{1,0:T(8,128)}) %reduce-scatter.5.cloned.1.call-update) | async-done | bytes 131088 | tf_op jit(solution)/shard_map/reduce_scatter | solution.py:114
  (73 shorter events, 22.4 us)
Async XLA Ops:
  6.5 146.9 %all-gather.9.cloned.1.call-start = ((), (), s32[]{:S(2)}) async-start(), calls=%async_computation.9 | async-start | bytes 2752512 | tf_op jit(solution)/shard_map/all_gather | solution.py:76
  91.9 5.4 copy-start.8
  92.0 5.5 copy-start.7
  92.0 5.6 copy-start.5
  92.0 5.7 copy-start.3
  97.1 234.6 %all-gather.5.cloned.1.call-start = ((), (), s32[]{:S(2)}) async-start(), calls=%async_computation.5 | async-start | bytes 4259840 | tf_op jit(solution)/shard_map/all_gather | solution.py:110
  120.7 2.0 copy-start.2
  120.7 2.3 copy-start
  123.0 0.9 copy-start.6
  123.0 1.0 copy-start.4
  148.0 54.7 %all-to-all-start = ((bf16[2,2,256,1792]{2,3,1,0:T(8,128)(2,1)}), bf16[2,2,256,1792]{2,3,1,0:T(8,128)(2,1)}, u32[]{:S(2)}, u32[]{:S(2)}) async-start(bf16[2,2,256,1792]{2,3,1,0:T(8,128)(2,1)} %pad_maximum_fusion), calls=%async_computation | async-start | bytes 7340032 | tf_op jit(solution)/shard_map/all_to_all | solution.py:74
  202.7 31.3 %all-to-all-start.2 = ((bf16[1,256,2,16,112]{1,4,2,0,3:T(8,128)(2,1)}), bf16[1,256,2,16,112]{1,4,2,0,3:T(8,128)(2,1)S(1)}, u32[]{:S(2)}, u32[]{:S(2)}) async-start(bf16[1,256,2,16,112]{1,4,2,0,3:T(8,128)(2,1)} %copy.51), calls=%async_computation.2 | async-start | bytes 3670016 | tf_op jit(solution)/shard_map/all_to_all | solution.py:83
  233.9 52.0 %all-to-all-start.1 = ((bf16[2,256,2,16,112]{1,4,2,0,3:T(8,128)(2,1)}), bf16[2,256,2,16,112]{1,4,2,0,3:T(8,128)(2,1)}, u32[]{:S(2)}, u32[]{:S(2)}) async-start(bf16[2,256,2,16,112]{1,4,2,0,3:T(8,128)(2,1)} %copy.45), calls=%async_computation.1 | async-start | bytes 7340032 | tf_op jit(solution)/shard_map/all_to_all | solution.py:82
  238.4 407.4 %reduce-scatter.3.cloned.1.call-start = ((), (), s32[]{:S(2)}) async-start(), calls=%async_computation.6 | async-start | bytes 8519680 | tf_op jit(solution)/shard_map/reduce_scatter | solution.py:114
  344.6 459.1 %all-gather.7.cloned.1.call-start = ((), (), s32[]{:S(2)}) async-start(), calls=%async_computation.7 | async-start | bytes 4259840 | tf_op jit(solution)/shard_map/all_gather | solution.py:110
  345.0 3.7 copy-start.1
  647.7 468.6 %reduce-scatter.5.cloned.1.call-start = ((), (), s32[]{:S(2)}) async-start(), calls=%async_computation.8 | async-start | bytes 8519680 | tf_op jit(solution)/shard_map/reduce_scatter | solution.py:114
Sparse Core Ops, SparseCore 0:
  97.2 30.3 all-gather.8
  129.3 202.3 all-gather.4
  344.7 301.1 reduce-scatter.2
  647.8 155.8 all-gather.6
  816.8 299.5 reduce-scatter.4
